TPU v7x, 128 devices: a whole 4x4x4 slice. The times are simulated.
128 devices in a mesh: ent: 32 (over x_hi, z, y), sec: 4 (over x_lo, core).
Axes of the slice: x: 4 (x_hi: 2, x_lo: 2; x = x_hi * 2 + x_lo), y: 4, z: 4, core: 2. Of those that a mesh axis runs over, the one named last changes fastest.
Arguments:
- features: bfloat16 [4096, 256], P('ent'), may hold values from -6 to 6
- theta: bfloat16 [256, 256], replicated, may hold values from -3 to 3
- section_weight: float32 [65536], P(('ent', 'sec')), may hold values from 0.5 to 2
- pair_rows: int32 [128, 32, 512], P(('ent', 'sec')), may hold values from 0 to 511
- pair_cols: int32 [128, 32, 512], P(('ent', 'sec')), may hold values from 0 to 127
- pair_counts: int32 [128, 32], P(('ent', 'sec')), may hold values from 0 to 512, as said below
- cotangent: bfloat16 [4096, 256], P('ent'), may hold values from -24 to 24
Outputs:
- activated: bfloat16 [4096, 256], P('ent')
- grad_features: bfloat16 [4096, 256], P('ent')
- grad_theta: float32 [256, 256], replicated
- grad_weight: float32 [65536], P(('ent', 'sec'))
Inputs may be any that keep to these rules, and one draw needn't show every extreme that they name: Only the first pair_counts[k, j] slots of shard k and block j are used; some shard uses all 512 slots of some block.
All inputs are finite; a program needn't handle non-finite values.
Results may differ from a plain program's by a relative error of at most 0.0059.
Values may be sent and summed in bfloat16 or wider, within the bound.
A program may use at most 64 MiB of HBM per device.

v0:
```python
import jax
import jax.numpy as jnp
from jax import lax
from jax.sharding import PartitionSpec as P


def hot_table(indices, live_slots, offset, table_width):
    hits = (indices - offset)[:, None] == jnp.arange(table_width, dtype=jnp.int32)[None, :]
    return (hits & live_slots[:, None]).astype(jnp.bfloat16)


def body(features, theta, section_weight, pair_rows, pair_cols, pair_counts, cotangent):
    ent_dev = features.shape[0]
    feature_width = features.shape[1]
    sec_dev = section_weight.shape[0]
    blocks_count = pair_rows.shape[1]
    slot_count = pair_rows.shape[2]
    own_block = lax.axis_index("ent")
    row_lists = pair_rows[0]
    col_lists = pair_cols[0]
    usable = jnp.arange(slot_count, dtype=jnp.int32)[None, :] < pair_counts[0][:, None]
    usable_float = usable.astype(jnp.float32)
    entity_index = jnp.arange(blocks_count, dtype=jnp.int32)[:, None] * ent_dev + col_lists
    local_degree = jax.ops.segment_sum(
        usable_float.reshape(-1), entity_index.reshape(-1), num_segments=blocks_count * ent_dev
    )
    entity_degree = lax.psum(local_degree, ("ent", "sec"))
    own_degree = lax.dynamic_slice_in_dim(entity_degree, own_block * ent_dev, ent_dev)
    entity_scale = lax.rsqrt(1.0 + own_degree)[:, None]
    sec_count = jax.ops.segment_sum(
        usable_float.reshape(-1), row_lists.reshape(-1), num_segments=sec_dev
    )
    section_scale = (section_weight / (1.0 + sec_count))[:, None]

    def entity_fold(running, incoming, start_row):
        row_count = incoming.shape[0]
        span_width = min(row_count, ent_dev)
        block_span = max(row_count // ent_dev, 1)
        offset = start_row

        def add_block(turn_index, accum):
            row_slots = lax.dynamic_index_in_dim(row_lists, turn_index, 0, keepdims=False)
            col_slots = lax.dynamic_index_in_dim(col_lists, turn_index, 0, keepdims=False)
            live_slots = lax.dynamic_index_in_dim(usable, turn_index, 0, keepdims=False)
            values = lax.dynamic_slice_in_dim(incoming, turn_index * span_width, span_width, 0)
            col_hot = hot_table(col_slots, live_slots, offset, span_width)
            row_hot = hot_table(row_slots, live_slots, 0, sec_dev)
            picked = jnp.dot(col_hot, values, preferred_element_type=jnp.float32).astype(
                jnp.bfloat16
            )
            return accum + jnp.einsum(
                "ps,pf->sf", row_hot, picked, preferred_element_type=jnp.float32
            )

        return lax.fori_loop(0, block_span, add_block, running)

    def entity_terms(messages, start_row):
        span_width = min(lax.axis_size("ent") * ent_dev, ent_dev)
        block_span = max(lax.axis_size("ent") * ent_dev // ent_dev, 1)
        offset = start_row

        def block_term(turn_index):
            row_slots = lax.dynamic_index_in_dim(row_lists, turn_index, 0, keepdims=False)
            col_slots = lax.dynamic_index_in_dim(col_lists, turn_index, 0, keepdims=False)
            live_slots = lax.dynamic_index_in_dim(usable, turn_index, 0, keepdims=False)
            row_hot = hot_table(row_slots, live_slots, 0, sec_dev)
            col_hot = hot_table(col_slots, live_slots, offset, span_width)
            picked = jnp.dot(row_hot, messages, preferred_element_type=jnp.float32).astype(
                jnp.bfloat16
            )
            return jnp.einsum("pw,pf->wf", col_hot, picked, preferred_element_type=jnp.float32)

        pieces = lax.map(block_term, jnp.arange(block_span, dtype=jnp.int32))
        return pieces.reshape(block_span * span_width, feature_width)

    def collect(messages):
        partial_sum = lax.psum_scatter(
            entity_terms(messages, jnp.int32(0)), "ent", scatter_dimension=0, tiled=True
        )
        return lax.psum(partial_sum, "sec")

    zero_sections = jnp.zeros((sec_dev, feature_width), jnp.float32)
    projected = jnp.dot(features, theta, preferred_element_type=jnp.float32)
    scaled = (entity_scale * projected).astype(jnp.bfloat16)
    gathered = entity_fold(
        zero_sections, lax.all_gather(scaled, "ent", axis=0, tiled=True), jnp.int32(0)
    )
    messages = (section_scale * gathered).astype(jnp.bfloat16)
    collected = collect(messages)
    preact = entity_scale * collected
    activated = jax.nn.silu(preact).astype(jnp.bfloat16)
    sigmoid_pre = jax.nn.sigmoid(preact)
    grad_pre = cotangent.astype(jnp.float32) * sigmoid_pre * (1.0 + preact * (1.0 - sigmoid_pre))
    back_scaled = (entity_scale * grad_pre).astype(jnp.bfloat16)
    back_gathered = entity_fold(
        zero_sections, lax.all_gather(back_scaled, "ent", axis=0, tiled=True), jnp.int32(0)
    )
    grad_weight = jnp.sum(gathered * back_gathered, axis=1) / (1.0 + sec_count)
    back_messages = (section_scale * back_gathered).astype(jnp.bfloat16)
    back_collected = collect(back_messages)
    grad_proj = (entity_scale * back_collected).astype(jnp.bfloat16)
    grad_features = lax.dot_general(
        grad_proj, theta, (((1,), (1,)), ((), ())), preferred_element_type=jnp.float32
    ).astype(jnp.bfloat16)
    local_theta = lax.dot_general(
        features, grad_proj, (((0,), (0,)), ((), ())), preferred_element_type=jnp.float32
    )
    grad_theta = lax.psum(local_theta, "ent")
    return (activated, grad_features, grad_theta, grad_weight)


def solution(mesh):
    placed = (
        P("ent", None),
        P(),
        P(("ent", "sec")),
        P(("ent", "sec"), None, None),
        P(("ent", "sec"), None, None),
        P(("ent", "sec"), None),
        P("ent", None),
    )
    return jax.shard_map(
        body,
        mesh=mesh,
        in_specs=placed,
        out_specs=(P("ent", None), P("ent", None), P(), P(("ent", "sec"))),
        check_vma=False,
    )
```

profile of v0, /device:TPU:0, one launch (start us, length us, event | category | flops | bytes accessed | tf_op | source)
XLA Modules:
  0.0 1644.0 jit_solution(5554662827985014451)
XLA Ops:
  9.2 113.5 %scatter_custom_fusion = f32[4096]{0:T(1024)S(1)} fusion(s32[16384]{0:T(1024)S(1)} %bitcast.81, f32[16384]{0:T(1024)S(1)} %bitcast.82, f32[]{:T(128)} %constant.131.clone.1), kind=kCustom, calls=%fused_computation.76 | custom fusion | flops 16384 | bytes 16388 | tf_op jit(solution)/shard_map/scatter-add | solution.py:24
  122.6 68.3 %psum.28 = f32[4096]{0:T(1024)S(1)} all-reduce(f32[4096]{0:T(1024)S(1)} %scatter_custom_fusion), channel_id=1, replica_groups=mesh['ent'=32,'sec'=4] {'ent','sec'}, use_global_device_ids=true, to_apply=%region_1.0 | all-reduce | flops 4096 | bytes 32768 | tf_op jit(solution)/shard_map/psum | solution.py:27
  193.5 113.4 %scatter_custom_fusion.1 = f32[512]{0:T(512)S(1)} fusion(s32[16384]{0:T(1024)S(1)} %bitcast.84, f32[16384]{0:T(1024)S(1)} %bitcast.83, f32[]{:T(128)} %constant.137.clone.1), kind=kCustom, calls=%fused_computation.78 | custom fusion | flops 16384 | bytes 2052 | tf_op jit(solution)/shard_map/scatter-add | solution.py:30
  307.7 79.9 %while.50 = (s32[]{:T(128)}, f32[512,256]{1,0:T(8,128)S(1)}, s32[32,512]{1,0:T(8,128)}, pred[32,512]{1,0:T(8,128)(4,1)S(1)}, s32[32,512]{1,0:T(8,128)}, /*index=...) while((s32[]{:T(128)}, f32[512,256]{1,0:T(8,128)S(1)}, ...), condition=%wide.region_4.5_spmd.clone, body=%wide.region_3.4_spmd.clone.sunk | while | flops 168820736 | bytes 1128617 | solution.py:55
  313.4 1.7 convolution_add_fusion.4
  315.9 1.7 convolution_add_fusion.4
  330.9 1.7 convolution_add_fusion.4
  333.4 1.7 convolution_add_fusion.4
  348.4 1.7 convolution_add_fusion.4
  350.9 1.7 convolution_add_fusion.4
  365.9 1.7 convolution_add_fusion.4
  368.4 1.7 convolution_add_fusion.4
  383.4 1.7 convolution_add_fusion.4
  385.9 1.7 convolution_add_fusion.4
  387.7 2.4 broadcast.21.clone
  390.2 144.5 %while.48 = (s32[]{:T(128)}, f32[32,128,256]{2,1,0:T(8,128)}, s32[32]{0:T(128)S(1)}, s32[32,512]{1,0:T(8,128)}, pred[32,512]{1,0:T(8,128)(4,1)S(1)}, /*index=5*/...) while((s32[]{:T(128)}, f32[32,128,256]{2,1,0:T(8,128)}, ...), condition=%wide.region_6.7_spmd, body=%wide.region_5.6_spmd.sunk | while | flops 168558592 | bytes 408219 | solution.py:73
  534.8 188.6 %reduce-scatter.3.cloned.1.call-done = f32[128,256]{1,0:T(8,128)} async-done(((f32[4096,256]{1,0:T(8,128)}), f32[128,256]{1,0:T(8,128)}) %reduce-scatter.3.cloned.1.call-update) | async-done | bytes 131088 | tf_op jit(solution)/shard_map/reduce_scatter | solution.py:77
  723.4 32.8 %all-reduce.4.cloned.1.call-done = f32[128,256]{1,0:T(8,128)} async-done(((f32[128,256]{1,0:T(8,128)}), f32[128,256]{1,0:T(8,128)}) %all-reduce.4.cloned.1.call-update) | async-done | bytes 131088 | tf_op jit(solution)/shard_map/psum | solution.py:80
  756.2 1.7 multiply_convert_fusion.3
  758.0 73.9 %all-gather.5.cloned.1.call-done = bf16[4096,256]{1,0:T(8,128)(2,1)} async-done(((bf16[128,256]{1,0:T(8,128)(2,1)}), bf16[4096,256]{1,0:T(8,128)(2,1)}) %all-gather.5.cloned.1.call-update) | async-done | bytes 2097168 | tf_op jit(solution)/shard_map/all_gather | solution.py:96
  831.9 79.9 %while.51 = (s32[]{:T(128)}, f32[512,256]{1,0:T(8,128)S(1)}, s32[32,512]{1,0:T(8,128)}, pred[32,512]{1,0:T(8,128)(4,1)S(1)}, s32[32,512]{1,0:T(8,128)}, /*index=...) while((s32[]{:T(128)}, f32[512,256]{1,0:T(8,128)S(1)}, ...), condition=%wide.region_10.11_spmd.clone, body=%wide.region_9.10_spmd.clone.sunk | while | flops 168820736 | bytes 1128617 | solution.py:55
  832.6 1.7 convolution_add_fusion.5
  842.6 1.7 convolution_add_fusion.5
  845.1 1.7 convolution_add_fusion.5
  912.0 2.4 broadcast.21
  914.4 144.5 %while.49 = (s32[]{:T(128)}, f32[32,128,256]{2,1,0:T(8,128)}, s32[32]{0:T(128)S(1)}, s32[32,512]{1,0:T(8,128)}, pred[32,512]{1,0:T(8,128)(4,1)S(1)}, /*index=5*/...) while((s32[]{:T(128)}, f32[32,128,256]{2,1,0:T(8,128)}, ...), condition=%wide.region_12.13_spmd, body=%wide.region_11.12_spmd.sunk | while | flops 168558592 | bytes 408219 | solution.py:73
  1059.0 190.6 %reduce-scatter.5.cloned.1.call-done = f32[128,256]{1,0:T(8,128)} async-done(((f32[4096,256]{1,0:T(8,128)}), f32[128,256]{1,0:T(8,128)}) %reduce-scatter.5.cloned.1.call-update) | async-done | bytes 131088 | tf_op jit(solution)/shard_map/reduce_scatter | solution.py:77
  1249.7 32.8 %all-reduce.6.cloned.1.call-done = f32[128,256]{1,0:T(8,128)} async-done(((f32[128,256]{1,0:T(8,128)}), f32[128,256]{1,0:T(8,128)}) %all-reduce.6.cloned.1.call-update) | async-done | bytes 131088 | tf_op jit(solution)/shard_map/psum | solution.py:80
  1282.5 1.9 convolution_bitcast_fusion
  1285.0 1.7 convolution_convert_fusion.4
  1286.8 348.6 %all-reduce.8.cloned.1.call-done = f32[256,256]{0,1:T(8,128)} async-done(((f32[256,256]{0,1:T(8,128)}), f32[256,256]{0,1:T(8,128)}) %all-reduce.8.cloned.1.call-update) | async-done | bytes 262160 | tf_op jit(solution)/shard_map/psum | solution.py:108
  1635.4 1.8 copy.11
  (474 shorter events, 307.0 us)
Async XLA Ops:
  7.2 183.8 %copy-start = (bf16[256,256]{1,0:T(8,128)(2,1)S(1)}, bf16[256,256]{1,0:T(8,128)(2,1)}, u32[]{:S(2)}) copy-start(bf16[256,256]{1,0:T(8,128)(2,1)} %param.16) | copy-start | bytes 393220
  7.2 300.5 %all-gather.3.cloned.1.call-start = ((), (), s32[]{:S(2)}) async-start(), calls=%async_computation.2 | async-start | bytes 2162688 | tf_op jit(solution)/shard_map/all_gather | solution.py:86
  192.6 530.7 %reduce-scatter.3.cloned.1.call-start = ((), (), s32[]{:S(2)}) async-start(), calls=%async_computation.3 | async-start | bytes 4325376 | tf_op jit(solution)/shard_map/reduce_scatter | solution.py:77
  390.1 366.0 %copy-start.2 = (bf16[128,256]{1,0:T(8,128)(2,1)S(1)}, bf16[128,256]{1,0:T(8,128)(2,1)}, u32[]{:S(2)}) copy-start(bf16[128,256]{1,0:T(8,128)(2,1)} %param.21) | copy-start | bytes 196612
  534.7 221.5 %all-reduce.4.cloned.1.call-start = ((), (), s32[]{:S(2)}) async-start(), calls=%async_computation.4 | async-start | bytes 262144 | tf_op jit(solution)/shard_map/psum | solution.py:80
  723.4 108.5 %all-gather.5.cloned.1.call-start = ((), (), s32[]{:S(2)}) async-start(), calls=%async_computation.5 | async-start | bytes 2162688 | tf_op jit(solution)/shard_map/all_gather | solution.py:96
  757.9 491.7 %reduce-scatter.5.cloned.1.call-start = ((), (), s32[]{:S(2)}) async-start(), calls=%async_computation.6 | async-start | bytes 4325376 | tf_op jit(solution)/shard_map/reduce_scatter | solution.py:77
  914.4 368.1 %copy-start.1 = (bf16[128,256]{1,0:T(8,128)(2,1)S(1)}, bf16[128,256]{1,0:T(8,128)(2,1)}, u32[]{:S(2)}) copy-start(bf16[128,256]{1,0:T(8,128)(2,1)} %param.15) | copy-start | bytes 196612
  1059.0 223.6 %all-reduce.6.cloned.1.call-start = ((), (), s32[]{:S(2)}) async-start(), calls=%async_computation.7 | async-start | bytes 262144 | tf_op jit(solution)/shard_map/psum | solution.py:80
  1249.7 385.8 %all-reduce.8.cloned.1.call-start = ((), (), s32[]{:S(2)}) async-start(), calls=%async_computation.8 | async-start | bytes 524288 | tf_op jit(solution)/shard_map/psum | solution.py:108
Sparse Core Ops, SparseCore 0:
  192.7 66.8 all-gather.2
  534.8 188.4 reduce-scatter.2
  725.8 30.3 all-reduce.3
  760.1 71.6 all-gather.4
  1059.1 190.4 reduce-scatter.4
  1252.1 30.3 all-reduce.5
  1285.6 349.7 all-reduce.7
where the time goes:
time: 1670 us; the launch traced here: 1640 us
  waiting for transfers between devices  867 us (52%)
  other arithmetic  231 us (14%)
  matrix products  191 us (11%)
  local copies, waits for them, and re-layouts  145 us (9%)
  loops' own time  126 us (8%)
  blocking collectives  68.3 us (4%)
    reduce_scatter x2, waiting for transfers between devices, collect(): lax.psum_scatter(entity_terms(messages, jnp.int32(0)), 'ent', scatter_dim...  379 us
    psum x1, waiting for transfers between devices, body(): grad_theta = lax.psum(local_theta, 'ent')  349 us
    another operation x2, loops' own time, entity_terms(): pieces = lax.map(block_term, jnp.arange(block_span, dtype=jnp.int32))  125 us
    scatter-add x1, other arithmetic, body(): jax.ops.segment_sum(usable_float.reshape(-1), entity_index.reshape(-1), n...  113 us
    scatter-add x1, other arithmetic, body(): jax.ops.segment_sum(usable_float.reshape(-1), row_lists.reshape(-1), num_...  113 us
    dot_general x64, matrix products, add_block(): jnp.einsum('ps,pf->sf', row_hot, picked, preferred_element_type=jnp.float32)  108 us
    dot_general x64, matrix products, block_term(): jnp.einsum('pw,pf->wf', col_hot, picked, preferred_element_type=jnp.float32)  77.7 us
    all_gather x1, waiting for transfers between devices, body(): lax.all_gather(back_scaled, 'ent', axis=0, tiled=True)  73.9 us
  transfers between devices with their start and end apart: 7, of which 6 were waited for; matrix products, arithmetic and copies ran while one was open for 7% of the time, Pallas kernels for 0%

commit v1 on v0

--- a/solution.py
+++ b/solution.py
@@ -77,7 +77,7 @@
         partial_sum = lax.psum_scatter(
             entity_terms(messages, jnp.int32(0)), "ent", scatter_dimension=0, tiled=True
         )
-        return lax.psum(partial_sum, "sec")
+        return jnp.sum(lax.all_gather(partial_sum, "sec"), axis=0)
 
     zero_sections = jnp.zeros((sec_dev, feature_width), jnp.float32)
     projected = jnp.dot(features, theta, preferred_element_type=jnp.float32)

time: 1670 us -> 1600 us (0.958)
  waiting for transfers between devices: 867 us -> 788 us
    psum x2 -> x0, waiting for transfers between devices: 65.6 us -> none  [collect(): return lax.psum(partial_sum, 'sec')]
  transfers between devices with their start and end apart: 7 -> 5, of which waited for: 6 -> 4; matrix products, arithmetic and copies ran while one was open for 7% -> 7% of each run, Pallas kernels for 0% -> 0%
where the time goes in v1:
time: 1600 us; the launch traced here: 1570 us
  waiting for transfers between devices  788 us (49%)
  other arithmetic  230 us (14%)
  matrix products  190 us (12%)
  local copies, waits for them, and re-layouts  145 us (9%)
  loops' own time  126 us (8%)
  blocking collectives  81.7 us (5%)
    reduce_scatter x2, waiting for transfers between devices, collect(): lax.psum_scatter(entity_terms(messages, jnp.int32(0)), 'ent', scatter_dim...  379 us
    psum x1, waiting for transfers between devices, body(): grad_theta = lax.psum(local_theta, 'ent')  342 us
    another operation x2, loops' own time, entity_terms(): pieces = lax.map(block_term, jnp.arange(block_span, dtype=jnp.int32))  125 us
    scatter-add x1, other arithmetic, body(): jax.ops.segment_sum(usable_float.reshape(-1), entity_index.reshape(-1), n...  113 us
    scatter-add x1, other arithmetic, body(): jax.ops.segment_sum(usable_float.reshape(-1), row_lists.reshape(-1), num_...  113 us
    dot_general x64, matrix products, add_block(): jnp.einsum('ps,pf->sf', row_hot, picked, preferred_element_type=jnp.float32)  108 us
    dot_general x64, matrix products, block_term(): jnp.einsum('pw,pf->wf', col_hot, picked, preferred_element_type=jnp.float32)  77.7 us
    psum x1, blocking collectives, body(): entity_degree = lax.psum(local_degree, ('ent', 'sec'))  68.3 us
  transfers between devices with their start and end apart: 5, of which 4 were waited for; matrix products, arithmetic and copies ran while one was open for 7% of the time, Pallas kernels for 0%

profile of v1, /device:TPU:0, one launch (start us, length us, event | category | flops | bytes accessed | tf_op | source)
XLA Modules:
  0.0 1574.7 jit_solution(8055403188114879739)
XLA Ops:
  9.2 113.5 %scatter_custom_fusion = f32[4096]{0:T(1024)S(1)} fusion(s32[16384]{0:T(1024)S(1)} %bitcast.85, f32[16384]{0:T(1024)S(1)} %bitcast.86, f32[]{:T(128)} %constant.131.clone.1), kind=kCustom, calls=%fused_computation.76 | custom fusion | flops 16384 | bytes 16388 | tf_op jit(solution)/shard_map/scatter-add | solution.py:24
  122.6 68.3 %psum.14 = f32[4096]{0:T(1024)S(1)} all-reduce(f32[4096]{0:T(1024)S(1)} %scatter_custom_fusion), channel_id=1, replica_groups=mesh['ent'=32,'sec'=4] {'ent','sec'}, use_global_device_ids=true, to_apply=%region_1.0 | all-reduce | flops 4096 | bytes 32768 | tf_op jit(solution)/shard_map/psum | solution.py:27
  193.5 113.4 %scatter_custom_fusion.1 = f32[512]{0:T(512)S(1)} fusion(s32[16384]{0:T(1024)S(1)} %bitcast.88, f32[16384]{0:T(1024)S(1)} %bitcast.87, f32[]{:T(128)} %constant.137.clone.1), kind=kCustom, calls=%fused_computation.78 | custom fusion | flops 16384 | bytes 2052 | tf_op jit(solution)/shard_map/scatter-add | solution.py:30
  307.7 79.9 %while.50 = (s32[]{:T(128)}, f32[512,256]{1,0:T(8,128)S(1)}, s32[32,512]{1,0:T(8,128)}, pred[32,512]{1,0:T(8,128)(4,1)S(1)}, s32[32,512]{1,0:T(8,128)}, /*index=...) while((s32[]{:T(128)}, f32[512,256]{1,0:T(8,128)S(1)}, ...), condition=%wide.region_4.5_spmd.clone, body=%wide.region_3.4_spmd.clone.sunk | while | flops 168820736 | bytes 1128617 | solution.py:55
  313.4 1.7 convolution_add_fusion.4
  315.9 1.7 convolution_add_fusion.4
  330.9 1.7 convolution_add_fusion.4
  333.4 1.7 convolution_add_fusion.4
  348.4 1.7 convolution_add_fusion.4
  350.9 1.7 convolution_add_fusion.4
  365.9 1.7 convolution_add_fusion.4
  368.4 1.7 convolution_add_fusion.4
  383.4 1.7 convolution_add_fusion.4
  385.9 1.7 convolution_add_fusion.4
  387.7 2.4 broadcast.21.clone
  390.1 144.5 %while.48 = (s32[]{:T(128)}, f32[32,128,256]{2,1,0:T(8,128)}, s32[32]{0:T(128)S(1)}, s32[32,512]{1,0:T(8,128)}, pred[32,512]{1,0:T(8,128)(4,1)S(1)}, /*index=5*/...) while((s32[]{:T(128)}, f32[32,128,256]{2,1,0:T(8,128)}, ...), condition=%wide.region_6.7_spmd, body=%wide.region_5.6_spmd.sunk | while | flops 168558592 | bytes 408219 | solution.py:73
  534.8 188.5 %reduce-scatter.3.cloned.1.call-done = f32[128,256]{1,0:T(8,128)} async-done(((f32[4096,256]{1,0:T(8,128)}), f32[128,256]{1,0:T(8,128)}) %reduce-scatter.3.cloned.1.call-update) | async-done | bytes 131088 | tf_op jit(solution)/shard_map/reduce_scatter | solution.py:77
  723.3 6.7 all-gather
  730.9 66.2 %all-gather.7.cloned.1.call-done = bf16[4096,256]{1,0:T(8,128)(2,1)} async-done(((bf16[128,256]{1,0:T(8,128)(2,1)}), bf16[4096,256]{1,0:T(8,128)(2,1)}) %all-gather.7.cloned.1.call-update) | async-done | bytes 2097168 | tf_op jit(solution)/shard_map/all_gather | solution.py:96
  797.1 79.9 %while.51 = (s32[]{:T(128)}, f32[512,256]{1,0:T(8,128)S(1)}, s32[32,512]{1,0:T(8,128)}, pred[32,512]{1,0:T(8,128)(4,1)S(1)}, s32[32,512]{1,0:T(8,128)}, /*index=...) while((s32[]{:T(128)}, f32[512,256]{1,0:T(8,128)S(1)}, ...), condition=%wide.region_10.11_spmd.clone, body=%wide.region_9.10_spmd.clone.sunk | while | flops 168820736 | bytes 1128617 | solution.py:55
  805.3 1.7 convolution_add_fusion.5
  807.8 1.7 convolution_add_fusion.5
  822.8 1.7 convolution_add_fusion.5
  825.3 1.7 convolution_add_fusion.5
  840.3 1.7 convolution_add_fusion.5
  857.8 1.7 convolution_add_fusion.5
  877.2 2.4 broadcast.21
  879.6 144.6 %while.49 = (s32[]{:T(128)}, f32[32,128,256]{2,1,0:T(8,128)}, s32[32]{0:T(128)S(1)}, s32[32,512]{1,0:T(8,128)}, pred[32,512]{1,0:T(8,128)(4,1)S(1)}, /*index=5*/...) while((s32[]{:T(128)}, f32[32,128,256]{2,1,0:T(8,128)}, ...), condition=%wide.region_12.13_spmd, body=%wide.region_11.12_spmd.sunk | while | flops 168558592 | bytes 408219 | solution.py:73
  1024.3 190.6 %reduce-scatter.5.cloned.1.call-done = f32[128,256]{1,0:T(8,128)} async-done(((f32[4096,256]{1,0:T(8,128)}), f32[128,256]{1,0:T(8,128)}) %reduce-scatter.5.cloned.1.call-update) | async-done | bytes 131088 | tf_op jit(solution)/shard_map/reduce_scatter | solution.py:77
  1214.9 6.7 all-gather.1
  1224.1 342.4 %all-reduce.2.cloned.1.call-done = f32[256,256]{0,1:T(8,128)} async-done(((f32[256,256]{0,1:T(8,128)}), f32[256,256]{0,1:T(8,128)}) %all-reduce.2.cloned.1.call-update) | async-done | bytes 262160 | tf_op jit(solution)/shard_map/psum | solution.py:108
  1566.4 1.8 copy.11
  (472 shorter events, 304.6 us)
Async XLA Ops:
  7.2 183.8 %copy-start = (bf16[256,256]{1,0:T(8,128)(2,1)S(1)}, bf16[256,256]{1,0:T(8,128)(2,1)}, u32[]{:S(2)}) copy-start(bf16[256,256]{1,0:T(8,128)(2,1)} %param.16) | copy-start | bytes 393220
  7.2 300.5 %all-gather.5.cloned.1.call-start = ((), (), s32[]{:S(2)}) async-start(), calls=%async_computation.2 | async-start | bytes 2162688 | tf_op jit(solution)/shard_map/all_gather | solution.py:86
  192.6 530.7 %reduce-scatter.3.cloned.1.call-start = ((), (), s32[]{:S(2)}) async-start(), calls=%async_computation.3 | async-start | bytes 4325376 | tf_op jit(solution)/shard_map/reduce_scatter | solution.py:77
  534.7 195.3 %copy-start.2 = (bf16[128,256]{1,0:T(8,128)(2,1)S(1)}, bf16[128,256]{1,0:T(8,128)(2,1)}, u32[]{:S(2)}) copy-start(bf16[128,256]{1,0:T(8,128)(2,1)} %param.21) | copy-start | bytes 196612
  534.7 262.3 %all-gather.7.cloned.1.call-start = ((), (), s32[]{:S(2)}) async-start(), calls=%async_computation.4 | async-start | bytes 2162688 | tf_op jit(solution)/shard_map/all_gather | solution.py:96
  730.9 484.0 %reduce-scatter.5.cloned.1.call-start = ((), (), s32[]{:S(2)}) async-start(), calls=%async_computation.5 | async-start | bytes 4325376 | tf_op jit(solution)/shard_map/reduce_scatter | solution.py:77
  1024.2 197.4 %copy-start.1 = (bf16[128,256]{1,0:T(8,128)(2,1)S(1)}, bf16[128,256]{1,0:T(8,128)(2,1)}, u32[]{:S(2)}) copy-start(bf16[128,256]{1,0:T(8,128)(2,1)} %param.15) | copy-start | bytes 196612
  1024.2 542.2 %all-reduce.2.cloned.1.call-start = ((), (), s32[]{:S(2)}) async-start(), calls=%async_computation.6 | async-start | bytes 524288 | tf_op jit(solution)/shard_map/psum | solution.py:108
Sparse Core Ops, SparseCore 0:
  192.7 66.8 all-gather.4
  534.8 188.3 reduce-scatter.2
  731.0 66.0 all-gather.6
  1024.4 190.4 reduce-scatter.4
  1222.7 343.6 all-reduce.1
